TPU v7x, 32 devices: a whole 2x2x4 slice. The times are simulated.
32 devices in a mesh: virt: 8 (over z, x), pair: 4 (over y, core).
Axes of the slice: x: 2, y: 2, z: 4, core: 2. Of those that a mesh axis runs over, the one named last changes fastest.
Arguments:
- amplitudes: bfloat16 [8, 1024, 2, 1024], P('pair'), may hold values from -6 to 6
- integrals: bfloat16 [2, 512, 8, 65536], P(None, None, None, ('virt', 'pair')), may hold values from -0.125 to 0.125
- virt_counts: int32 [8], replicated, may hold values from 32 to 64, as said below
- pair_counts: int32 [8], replicated, may hold values from 512 to 1024, as said below
- pair_list: int32 [8, 1024, 2], P('pair'), may hold values from 0 to 99
- eps_occ: float32 [100], replicated, may hold values from -2 to -0.3
- eps_virt: float32 [512], replicated, may hold values from 0.3 to 4
Outputs:
- update: bfloat16 [8, 1024, 32768], P('pair', None, 'virt')
- pair_energy: float32 [8, 1024], P('pair', 'virt')
Inputs may be any that keep to these rules, and one draw needn't show every extreme that they name: virt_counts[0] = 64; every count is at least 32. `pair_counts`: some pair symmetry has exactly 1024 pairs; every count is at least 512.
All inputs are finite; a program needn't handle non-finite values.
Results may differ from a plain program's by a relative error of at most 0.001.
Values may be sent and summed in bfloat16 or wider, within the bound.
A program may use at most 192 MiB of HBM per device.

v0:
```python
import jax
import jax.numpy as jnp
from jax import lax
from jax.sharding import PartitionSpec as P

IRREPS = 8
NV = 512
BLK = 64
CS = 16
SLABS = 2


def pick_counts(irrep_ids, table):
    onehot = irrep_ids[..., None] == jnp.arange(table.shape[0], dtype=jnp.int32)
    return jnp.sum(jnp.where(onehot, table, 0), axis=-1)


def shards(amplitudes, integrals, virt_counts, pair_counts, pair_list, eps_occ, eps_virt):
    local_irreps = amplitudes.shape[0]
    rows = amplitudes.shape[1]
    width = amplitudes.shape[3]
    n_virt = lax.axis_size("virt")
    n_pair = lax.axis_size("pair")
    a_local = NV // n_virt
    irrep_ids = lax.axis_index("pair") * local_irreps + jnp.arange(local_irreps, dtype=jnp.int32)
    slots = jnp.arange(BLK, dtype=jnp.int32)
    live_d = slots[None, :] < pick_counts(irrep_ids, virt_counts)[:, None]
    dmask = jnp.tile(live_d, (1, CS)).astype(jnp.bfloat16)
    masked = amplitudes * dmask[:, None, None, :]
    ladder = jnp.zeros((local_irreps, rows, a_local, BLK), jnp.float32)
    for s in range(SLABS):
        piece = integrals[s]
        moved = lax.all_to_all(
            lax.all_to_all(piece, "virt", split_axis=0, concat_axis=2, tiled=True),
            "pair",
            split_axis=1,
            concat_axis=2,
            tiled=True,
        )
        moved = moved.reshape(a_local, local_irreps, n_pair, n_virt, -1)
        moved = jnp.transpose(moved, (0, 1, 3, 2, 4)).reshape(a_local, local_irreps, BLK, width)
        ladder = ladder + jnp.einsum(
            "hrk,ahsk->hras", masked[:, :, s, :], moved, preferred_element_type=jnp.float32
        )
    a_global = lax.axis_index("virt") * a_local + jnp.arange(a_local, dtype=jnp.int32)
    a_irrep = a_global // BLK
    a_slot = a_global % BLK
    live_a = a_slot < pick_counts(a_irrep, virt_counts)
    eps_a = lax.dynamic_slice_in_dim(eps_virt, lax.axis_index("virt") * a_local, a_local)
    b_irrep = jnp.bitwise_xor(a_irrep[None, :], irrep_ids[:, None])
    b_onehot = (b_irrep[..., None] == jnp.arange(IRREPS, dtype=jnp.int32)).astype(jnp.float32)
    eps_table = eps_virt.reshape(IRREPS, BLK)
    eps_b = jnp.einsum("hag,gs->has", b_onehot, eps_table, precision=lax.Precision.HIGHEST)
    live_b = slots[None, None, :] < pick_counts(b_irrep, virt_counts)[..., None]
    occ_onehot = pair_list[..., None] == jnp.arange(eps_occ.shape[0], dtype=jnp.int32)
    occ_terms = jnp.sum(jnp.where(occ_onehot, eps_occ, 0.0), axis=-1)
    occ = occ_terms[:, :, 0] + occ_terms[:, :, 1]
    live_rows = (
        jnp.arange(rows, dtype=jnp.int32)[None, :] < pick_counts(irrep_ids, pair_counts)[:, None]
    )
    denom = (eps_a[None, :, None] + eps_b)[:, None, :, :] - occ[:, :, None, None]
    live = live_rows[:, :, None, None] & live_a[None, None, :, None] & live_b[:, None, :, :]
    ratio = jnp.where(live, ladder / denom, jnp.zeros_like(ladder))
    update = ratio.astype(jnp.bfloat16).reshape(local_irreps, rows, a_local * BLK)
    partial_value = jnp.sum(ratio * ladder, axis=(2, 3)) / (NV * BLK)
    energy = lax.psum_scatter(partial_value, "virt", scatter_dimension=1, tiled=True)
    return (update, energy)


def solution(mesh):
    placed = (
        P("pair", None, None, None),
        P(None, None, None, ("virt", "pair")),
        P(),
        P(),
        P("pair", None, None),
        P(),
        P(),
    )
    return jax.shard_map(
        shards,
        mesh=mesh,
        in_specs=placed,
        out_specs=(P("pair", None, "virt"), P("pair", "virt")),
        check_vma=False,
    )
```

profile of v0, /device:TPU:0, one launch (start us, length us, event | category | flops | bytes accessed | tf_op | source)
XLA Modules:
  0.0 1328.9 jit_solution(8190828221373560222)
XLA Ops:
  7.2 18.4 %slice_bitcast_fusion = (bf16[512,8,2048]{2,1,0:T(8,128)(2,1)S(1)}, bf16[512,8,2048]{2,1,0:T(8,128)(2,1)}) fusion(bf16[2,512,8,2048]{3,2,1,0:T(8,128)(2,1)} %param.8), kind=kLoop, calls=%fused_computation.6 | loop fusion | bytes 67108864 | tf_op jit(solution)/shard_map/squeeze | solution.py:32
  25.6 370.0 %all_to_all.66 = bf16[512,8,2048]{2,1,0:T(8,128)(2,1)} all-to-all(bf16[512,8,2048]{2,1,0:T(8,128)(2,1)S(1)} %get-tuple-element.14), channel_id=1, replica_groups=mesh['virt'=8,'pair'=4] {'virt'}, dimensions={0} | all-to-all | bytes 33554432 | tf_op jit(solution)/shard_map/all_to_all | solution.py:34
  395.6 5.8 all-to-all-start
  401.3 18.7 %copy.53 = bf16[8,64,8,2048]{3,0,2,1:T(8,128)(2,1)} copy(bf16[8,64,8,2048]{3,2,1,0:T(8,128)(2,1)} %bitcast.65) | data formatting | bytes 33554432 | tf_op jit(solution)/shard_map/all_to_all | solution.py:34
  420.0 25.6 %all_to_all.58 = bf16[64,8,16384]{2,1,0:T(8,128)(2,1)} reshape(bf16[64,8,8,2048]{3,2,1,0:T(8,128)(2,1)} %bitcast.66) | data formatting | bytes 33554432 | tf_op jit(solution)/shard_map/all_to_all | solution.py:34
  445.6 18.5 %copy.38 = bf16[64,8,16384]{2,0,1:T(8,128)(2,1)} copy(bf16[64,8,16384]{2,1,0:T(8,128)(2,1)} %all_to_all.58) | data formatting | bytes 33554432 | tf_op jit(solution)/shard_map/all_to_all | solution.py:34
  464.1 299.2 %all-to-all-done = bf16[512,8,2048]{2,1,0:T(8,128)(2,1)} async-done(((bf16[512,8,2048]{2,1,0:T(8,128)(2,1)}), bf16[512,8,2048]{2,1,0:T(8,128)(2,1)}, u32[]{:S(2)}, u32[]{:S(2)}) %all-to-all-start) | async-done | bytes 16777248 | tf_op jit(solution)/shard_map/all_to_all | solution.py:34
  763.3 7.0 all-to-all-start.3
  770.2 18.7 %copy.54 = bf16[8,64,8,2048]{3,0,2,1:T(8,128)(2,1)} copy(bf16[8,64,8,2048]{3,2,1,0:T(8,128)(2,1)} %bitcast.4) | data formatting | bytes 33554432 | tf_op jit(solution)/shard_map/all_to_all | solution.py:34
  788.9 25.6 %all_to_all.51 = bf16[64,8,16384]{2,1,0:T(8,128)(2,1)} reshape(bf16[64,8,8,2048]{3,2,1,0:T(8,128)(2,1)} %bitcast.67) | data formatting | bytes 33554432 | tf_op jit(solution)/shard_map/all_to_all | solution.py:34
  814.5 18.5 %copy.34 = bf16[64,8,16384]{2,0,1:T(8,128)(2,1)} copy(bf16[64,8,16384]{2,1,0:T(8,128)(2,1)} %all_to_all.51) | data formatting | bytes 33554432 | tf_op jit(solution)/shard_map/all_to_all | solution.py:34
  833.1 120.2 %all-to-all-done.3 = bf16[64,8,16384]{2,0,1:T(8,128)(2,1)} async-done(((bf16[64,8,16384]{2,0,1:T(8,128)(2,1)}), bf16[64,8,16384]{2,0,1:T(8,128)(2,1)}, u32[]{:S(2)}, u32[]{:S(2)}) %all-to-all-start.3) | async-done | bytes 16777248 | tf_op jit(solution)/shard_map/all_to_all | solution.py:33
  953.2 7.0 all-to-all-start.1
  960.2 0.2 reduce-scatter.4.cloned.1.call-start
  961.0 0.9 fusion.2
  962.4 0.2 convolution_add_fusion.1
  962.8 9.3 copy_multiply_fusion
  972.0 8.0 copy.39
  980.0 10.4 copy.48
  990.4 14.1 %copy.40 = bf16[64,2,8,4,2048]{4,3,2,0,1:T(4,128)(2,1)} copy(bf16[64,2,8,4,2048]{4,2,0,3,1:T(8,128)(2,1)S(1)} %bitcast.69) | data formatting | bytes 33554432 | tf_op jit(solution)/shard_map/transpose | solution.py:41
  1004.6 23.7 %reshape.187 = bf16[64,2,64,1024]{3,2,0,1:T(8,128)(2,1)} reshape(bf16[64,2,8,4,2048]{4,3,2,0,1:T(4,128)(2,1)} %copy.40) | data formatting | bytes 33554432 | tf_op jit(solution)/shard_map/reshape | solution.py:41
  1028.3 115.0 %all-to-all-done.1 = bf16[64,8,16384]{2,0,1:T(8,128)(2,1)} async-done(((bf16[64,8,16384]{2,0,1:T(8,128)(2,1)}), bf16[64,8,16384]{2,0,1:T(8,128)(2,1)}, u32[]{:S(2)}, u32[]{:S(2)}) %all-to-all-start.1) | async-done | bytes 16777248 | tf_op jit(solution)/shard_map/all_to_all | solution.py:33
  1143.2 8.0 copy.35
  1151.2 10.4 copy.47
  1161.7 14.1 %copy.36 = bf16[64,2,8,4,2048]{4,3,2,0,1:T(4,128)(2,1)} copy(bf16[64,2,8,4,2048]{4,2,0,3,1:T(8,128)(2,1)S(1)} %bitcast.71) | data formatting | bytes 33554432 | tf_op jit(solution)/shard_map/transpose | solution.py:41
  1175.8 23.7 %reshape.185 = bf16[64,2,64,1024]{3,2,0,1:T(8,128)(2,1)} reshape(bf16[64,2,8,4,2048]{4,3,2,0,1:T(4,128)(2,1)} %copy.36) | data formatting | bytes 33554432 | tf_op jit(solution)/shard_map/reshape | solution.py:41
  1199.5 26.7 %fusion.1 = f32[2,1024,64,64]{1,3,2,0:T(8,128)} fusion(bf16[64,2,64,1024]{3,2,0,1:T(8,128)(2,1)} %reshape.185, bf16[2,1024,2,1024]{3,1,0,2:T(8,128)(2,1)} %copy_multiply_fusion), kind=kOutput, calls=%fused_computation.11 | convolution fusion | flops 17179869184 | bytes 54525952 | tf_op jit(solution)/shard_map/hrk,ahsk->hras/dot_general | solution.py:42
  1226.2 32.0 %multiply_reduce_fusion = (f32[2,1024]{1,0:T(2,128)S(1)}, bf16[2,1024,64,64]{1,3,2,0:T(8,128)(2,1)}) fusion(f32[2,1024]{1,0:T(2,128)S(1)} %bitcast.75, f32[2,64,64]{2,1,0:T(8,128)S(1)} %convolution_add_fusion.1, pred[2,64,64]{2,1,0:T(8,128)(4,1)S(1)} %iota_compare_fusion, pred[2,1024,64]{1,2,0:T(8,128)(4,1)S(1)} %broadcast_and_fusion, ...), kind=kOutput, calls=%fused_computation | convolution fusion | flops 17246976000 | bytes 71491584 | tf_op jit(solution)/shard_map/hrk,ahsk->hras/dot_general | solution.py:42
  1258.2 1.0 copy.44
  1259.2 21.2 %copy.41 = bf16[2,1024,4096]{2,1,0:T(8,128)(2,1)} copy(bf16[2,1024,4096]{1,2,0:T(8,128)(2,1)} %bitcast.72) | data formatting | bytes 33554432
  1280.5 40.1 %reduce-scatter.4.cloned.1.call-done = f32[128,2]{1,0:T(8,128)} async-done(((f32[1024,2]{1,0:T(8,128)}), f32[128,2]{1,0:T(8,128)}) %reduce-scatter.4.cloned.1.call-update) | async-done | bytes 1040
  1320.6 1.5 copy.45
  (29 shorter events, 1.1 us)
Async XLA Ops:
  395.6 367.7 %all-to-all-start = ((bf16[512,8,2048]{2,1,0:T(8,128)(2,1)}), bf16[512,8,2048]{2,1,0:T(8,128)(2,1)}, u32[]{:S(2)}, u32[]{:S(2)}) async-start(bf16[512,8,2048]{2,1,0:T(8,128)(2,1)} %get-tuple-element.15), calls=%async_computation | async-start | bytes 33554432 | tf_op jit(solution)/shard_map/all_to_all | solution.py:34
  763.3 190.0 %all-to-all-start.3 = ((bf16[64,8,16384]{2,0,1:T(8,128)(2,1)}), bf16[64,8,16384]{2,0,1:T(8,128)(2,1)}, u32[]{:S(2)}, u32[]{:S(2)}) async-start(bf16[64,8,16384]{2,0,1:T(8,128)(2,1)} %copy.38), calls=%async_computation.3 | async-start | bytes 33554432 | tf_op jit(solution)/shard_map/all_to_all | solution.py:33
  833.0 127.4 %copy-start.1 = (f32[512]{0:T(512)S(1)}, f32[512]{0:T(512)}, u32[]{:S(2)}) copy-start(f32[512]{0:T(512)} %param.13) | copy-start | bytes 6148
  833.0 127.6 %copy-start.2 = (s32[8]{0:T(128)S(1)}, s32[8]{0:T(128)}, u32[]{:S(2)}) copy-start(s32[8]{0:T(128)} %param.9) | copy-start | bytes 100
  833.0 127.6 %copy-start.4 = (s32[8]{0:T(128)S(1)}, s32[8]{0:T(128)}, u32[]{:S(2)}) copy-start(s32[8]{0:T(128)} %param.10) | copy-start | bytes 100
  833.0 127.9 %copy-start = (s32[2,1024,2]{1,2,0:T(2,128)S(1)}, s32[2,1024,2]{1,2,0:T(2,128)}, u32[]{:S(2)}) copy-start(s32[2,1024,2]{1,2,0:T(2,128)} %param.11) | copy-start | bytes 49156
  833.0 127.9 %copy-start.3 = (f32[100]{0:T(128)S(1)}, f32[100]{0:T(128)}, u32[]{:S(2)}) copy-start(f32[100]{0:T(128)} %param.12) | copy-start | bytes 1204
  953.2 190.0 %all-to-all-start.1 = ((bf16[64,8,16384]{2,0,1:T(8,128)(2,1)}), bf16[64,8,16384]{2,0,1:T(8,128)(2,1)}, u32[]{:S(2)}, u32[]{:S(2)}) async-start(bf16[64,8,16384]{2,0,1:T(8,128)(2,1)} %copy.34), calls=%async_computation.1 | async-start | bytes 33554432 | tf_op jit(solution)/shard_map/all_to_all | solution.py:33
  960.2 360.4 %reduce-scatter.4.cloned.1.call-start = ((), (), s32[]{:S(2)}) async-start(), calls=%async_computation.5 | async-start | bytes 589824
Sparse Core Ops, SparseCore 0:
  1259.4 61.1 reduce-scatter.3
where the time goes:
time: 1330 us
  waiting for transfers between devices  574 us (43%)
  blocking collectives  370 us (28%)
  local copies, waits for them, and re-layouts  280 us (21%)
  matrix products  59 us (4%)
  starting transfers between devices  19.9 us (1%)
  between operations  14.2 us (1%)
    all_to_all x1, blocking collectives, shards(): lax.all_to_all(piece, 'virt', split_axis=0, concat_axis=2, tiled=True)  370 us
    all_to_all x1, waiting for transfers between devices, shards(): lax.all_to_all(piece, 'virt', split_axis=0, concat_axis=2, tiled=True)  299 us
    all_to_all x2, waiting for transfers between devices, shards(): lax.all_to_all(lax.all_to_all(piece, 'virt', split_axis=0, concat_axis=2,...  235 us
    all_to_all x6, local copies, waits for them, and re-layouts, shards(): lax.all_to_all(piece, 'virt', split_axis=0, concat_axis=2, tiled=True)  126 us
    dot_general x2, matrix products, shards(): jnp.einsum('hrk,ahsk->hras', masked[:, :, s, :], moved, preferred_element...  58.7 us
    reshape x2, local copies, waits for them, and re-layouts, shards(): jnp.transpose(moved, (0, 1, 3, 2, 4))  47.4 us
    unnamed x16, local copies, waits for them, and re-layouts  44.6 us
    unnamed x2, waiting for transfers between devices  40.1 us
  transfers between devices with their start and end apart: 4, of which 4 were waited for; matrix products, arithmetic and copies ran while one was open for 12% of the time, Pallas kernels for 0%

commit v1 on v0

--- a/solution.py
+++ b/solution.py
@@ -1,6 +1,10 @@
+import functools
+
 import jax
 import jax.numpy as jnp
 from jax import lax
+from jax.experimental import pallas as pl
+from jax.experimental.pallas import tpu as pltpu
 from jax.sharding import PartitionSpec as P
 
 IRREPS = 8
@@ -8,6 +12,7 @@
 BLK = 64
 CS = 16
 SLABS = 2
+MESH = pl.DeviceIdType.MESH
 
 
 def pick_counts(irrep_ids, table):
@@ -67,6 +72,238 @@
     return (update, energy)
 
 
+def flip_bits(index, pattern, count):
+    flipped = 0
+    weight = 1
+    while weight < count:
+        bit = (index // weight) % 2
+        mine = (pattern // weight) % 2
+        flipped = flipped + weight * (bit + mine - 2 * bit * mine)
+        weight *= 2
+    return flipped
+
+
+def ladder_kernel(
+    n_virt, n_pair, irreps_here, a_local, parts_sb,
+    eri_ref, amps_ref, rows_ref, occ_ref, sort_in_ref, sort_out_ref,
+    got_ref, recv_ref, energy_ref,
+    x_buf, stage, y_buf, out_buf,
+    x_sem, y_sem, own_sem, send_sem, recv_sem, out_sem, got_sem,
+):
+    me_v = lax.axis_index("virt")
+    me_p = lax.axis_index("pair")
+    slabs = eri_ref.shape[0]
+    loc = eri_ref.shape[2]
+    irreps = irreps_here * n_pair
+    ks = amps_ref.shape[2]
+    nrows = amps_ref.shape[3]
+    sort_rows = sort_in_ref.shape[0]
+    a_sort = sort_rows // irreps
+    sb_here = n_pair * parts_sb
+    chunk_rows = a_local * irreps
+    tile_n = 512
+    tile_r = 256
+
+    barrier = pltpu.get_barrier_semaphore()
+    for d in range(1, n_pair):
+        pl.semaphore_signal(barrier, inc=1, device_id=(me_v, flip_bits(me_p, d, n_pair)), device_id_type=MESH)
+    for d in range(1, n_virt):
+        pl.semaphore_signal(barrier, inc=1, device_id=(flip_bits(me_v, d, n_virt), me_p), device_id_type=MESH)
+    pl.semaphore_wait(barrier, n_pair - 1 + n_virt - 1)
+
+    def target(t):
+        return flip_bits(me_v, n_virt - 1 - t, n_virt)
+
+    def pair_copy(t, d):
+        peer = flip_bits(me_p, d, n_pair)
+        return pltpu.make_async_remote_copy(
+            src_ref=stage.at[t % 2, peer],
+            dst_ref=recv_ref.at[t, me_p],
+            send_sem=send_sem.at[t % 2, d - 1],
+            recv_sem=recv_sem.at[t, d - 1],
+            device_id=(me_v, peer),
+            device_id_type=MESH,
+        )
+
+    def own_copy(t):
+        return pltpu.make_async_copy(stage.at[t % 2, me_p], recv_ref.at[t, me_p], own_sem.at[t % 2])
+
+    def out_copy(t):
+        dest = target(t)
+        if t == n_virt - 1:
+            return pltpu.make_async_copy(out_buf.at[t], got_ref.at[:, :, me_v], own_sem.at[2])
+        return pltpu.make_async_remote_copy(
+            src_ref=out_buf.at[t],
+            dst_ref=got_ref.at[:, :, me_v],
+            send_sem=out_sem.at[t],
+            recv_sem=got_sem.at[t],
+            device_id=(dest, me_p),
+            device_id_type=MESH,
+        )
+
+    def prepare(t):
+        dest = target(t)
+        load = pltpu.make_async_copy(
+            eri_ref.at[:, pl.ds(pl.multiple_of(dest * chunk_rows, chunk_rows), chunk_rows), :], x_buf, x_sem
+        )
+        load.start()
+        load.wait()
+
+        def sort_tile(n, carry):
+            cols = pl.ds(pl.multiple_of(n * tile_n, tile_n), tile_n)
+            for s in range(slabs):
+                for q in range(a_local // a_sort):
+                    block = x_buf[s, q * sort_rows : (q + 1) * sort_rows, cols]
+                    sorted_rows = jnp.dot(
+                        sort_in_ref[...], block, preferred_element_type=jnp.float32
+                    ).astype(jnp.bfloat16)
+                    for h in range(irreps):
+                        stage[
+                            t % 2, h // irreps_here, h % irreps_here, s, q * a_sort : (q + 1) * a_sort, cols
+                        ] = sorted_rows[h * a_sort : (h + 1) * a_sort]
+            return carry
+
+        lax.fori_loop(0, loc // tile_n, sort_tile, 0)
+        for d in range(1, n_pair):
+            pair_copy(t, d).start()
+        own_copy(t).start()
+
+    def compute(t):
+        dest = target(t)
+        load = pltpu.make_async_copy(recv_ref.at[t], y_buf, y_sem)
+        load.start()
+        load.wait()
+        for hh in range(irreps_here):
+
+            def tile(n, carry):
+                cols = pl.ds(pl.multiple_of(n * tile_r, tile_r), tile_r)
+                ladder = None
+                for s in range(slabs):
+                    left = jnp.concatenate(
+                        [
+                            y_buf[p, hh, s, :, j * ks : (j + 1) * ks]
+                            for p in range(n_pair)
+                            for j in range(parts_sb)
+                        ],
+                        axis=0,
+                    )
+                    term = jnp.dot(left, amps_ref[hh, s, :, cols], preferred_element_type=jnp.float32)
+                    ladder = term if ladder is None else ladder + term
+                base = rows_ref[dest, :, hh : hh + 1]
+                live = rows_ref[dest, :, irreps_here + hh : irreps_here + hh + 1]
+                occ = occ_ref[hh : hh + 1, cols]
+                live_r = occ_ref[irreps_here + hh : irreps_here + hh + 1, cols]
+                denom = base - occ
+                ratio = jnp.where(live * live_r > 0.5, ladder / denom, 0.0)
+                energy_ref[hh : hh + 1, cols] += jnp.sum(ratio * ladder, axis=0, keepdims=True)
+                update = jnp.dot(
+                    sort_out_ref[...], ratio.astype(jnp.bfloat16), preferred_element_type=jnp.float32
+                ).astype(jnp.bfloat16)
+                out_buf[t, hh, :, :, cols] = update.reshape(a_local, sb_here, tile_r)
+                return carry
+
+            lax.fori_loop(0, nrows // tile_r, tile, 0)
+        out_copy(t).start()
+
+    energy_ref[...] = jnp.zeros_like(energy_ref)
+    prepare(0)
+    prepare(1)
+    for t in range(n_virt):
+        for d in range(1, n_pair):
+            pair_copy(t, d).wait_recv()
+        own_copy(t).wait()
+        compute(t)
+        for d in range(1, n_pair):
+            pair_copy(t, d).wait_send()
+        if t + 2 < n_virt:
+            prepare(t + 2)
+    for t in range(n_virt):
+        out_copy(t).wait()
+
+
+def fused_shards(amplitudes, integrals, virt_counts, pair_counts, pair_list, eps_occ, eps_virt):
+    irreps_here, rows, slabs, ks = amplitudes.shape
+    n_virt = lax.axis_size("virt")
+    n_pair = lax.axis_size("pair")
+    nv = integrals.shape[1]
+    irreps = integrals.shape[2]
+    loc = integrals.shape[3]
+    a_local = nv // n_virt
+    parts_sb = loc // ks
+    sb_here = n_pair * parts_sb
+    me_v = lax.axis_index("virt")
+    irrep_ids = lax.axis_index("pair") * irreps_here + jnp.arange(irreps_here, dtype=jnp.int32)
+    slots = jnp.arange(BLK, dtype=jnp.int32)
+    live_d = slots[None, :] < pick_counts(irrep_ids, virt_counts)[:, None]
+    dmask = jnp.tile(live_d, (1, ks // BLK)).astype(jnp.bfloat16)
+    masked = amplitudes * dmask[:, None, None, :]
+    amps = jnp.transpose(masked, (0, 2, 3, 1))
+
+    a_index = jnp.arange(nv, dtype=jnp.int32)
+    a_irrep = a_index // BLK
+    live_virt = (slots[None, :] < virt_counts[:, None]).astype(jnp.float32)
+    b_irrep = jnp.bitwise_xor(a_irrep[None, :], irrep_ids[:, None])
+    b_onehot = (b_irrep[..., None] == jnp.arange(irreps, dtype=jnp.int32)).astype(jnp.float32)
+    eps_here = lax.dynamic_slice_in_dim(eps_virt.reshape(irreps, BLK), me_v * sb_here, sb_here, axis=1)
+    live_here = lax.dynamic_slice_in_dim(live_virt, me_v * sb_here, sb_here, axis=1)
+    eps_b = jnp.einsum("hag,gs->hsa", b_onehot, eps_here, precision=lax.Precision.HIGHEST)
+    live_b = jnp.einsum("hag,gs->hsa", b_onehot, live_here, precision=lax.Precision.HIGHEST)
+    base = eps_virt[None, None, :] + eps_b
+    live = live_virt.reshape(-1)[None, None, :] * live_b
+    cols = jnp.concatenate([base, live], axis=0)
+    cols = cols.reshape(2 * irreps_here, sb_here, n_virt, a_local)
+    cols = jnp.transpose(cols, (2, 1, 3, 0)).reshape(n_virt, sb_here * a_local, 2 * irreps_here)
+
+    occ_onehot = pair_list[..., None] == jnp.arange(eps_occ.shape[0], dtype=jnp.int32)
+    occ_terms = jnp.sum(jnp.where(occ_onehot, eps_occ, 0.0), axis=-1)
+    occ = occ_terms[:, :, 0] + occ_terms[:, :, 1]
+    live_rows = jnp.arange(rows, dtype=jnp.int32)[None, :] < pick_counts(irrep_ids, pair_counts)[:, None]
+    occ_live = jnp.concatenate([occ, live_rows.astype(jnp.float32)], axis=0)
+
+    a_sort = 32
+    n_in = a_sort * irreps
+    i_in = jnp.arange(n_in, dtype=jnp.int32)
+    from_in = (i_in % a_sort) * irreps + i_in // a_sort
+    sort_in = (from_in[:, None] == i_in[None, :]).astype(jnp.bfloat16)
+    i_out = jnp.arange(a_local * sb_here, dtype=jnp.int32)
+    from_out = (i_out % sb_here) * a_local + i_out // sb_here
+    sort_out = (from_out[:, None] == i_out[None, :]).astype(jnp.bfloat16)
+
+    eri = integrals.reshape(slabs, nv * irreps, loc)
+    vmem = pl.BlockSpec(memory_space=pltpu.VMEM)
+    hbm = pl.BlockSpec(memory_space=pl.ANY)
+    got, _, energy = pl.pallas_call(
+        functools.partial(ladder_kernel, n_virt, n_pair, irreps_here, a_local, parts_sb),
+        out_shape=(
+            jax.ShapeDtypeStruct((irreps_here, a_local, n_virt, sb_here, rows), jnp.bfloat16),
+            jax.ShapeDtypeStruct((n_virt, n_pair, irreps_here, slabs, a_local, loc), jnp.bfloat16),
+            jax.ShapeDtypeStruct((irreps_here, rows), jnp.float32),
+        ),
+        in_specs=[hbm, vmem, vmem, vmem, vmem, vmem],
+        out_specs=(hbm, hbm, vmem),
+        scratch_shapes=[
+            pltpu.VMEM((slabs, a_local * irreps, loc), jnp.bfloat16),
+            pltpu.VMEM((2, n_pair, irreps_here, slabs, a_local, loc), jnp.bfloat16),
+            pltpu.VMEM((n_pair, irreps_here, slabs, a_local, loc), jnp.bfloat16),
+            pltpu.VMEM((n_virt, irreps_here, a_local, sb_here, rows), jnp.bfloat16),
+            pltpu.SemaphoreType.DMA,
+            pltpu.SemaphoreType.DMA,
+            pltpu.SemaphoreType.DMA((3,)),
+            pltpu.SemaphoreType.DMA((2, n_pair - 1)),
+            pltpu.SemaphoreType.DMA((n_virt, n_pair - 1)),
+            pltpu.SemaphoreType.DMA((n_virt,)),
+            pltpu.SemaphoreType.DMA((n_virt,)),
+        ],
+        compiler_params=pltpu.CompilerParams(
+            collective_id=0, has_side_effects=True, vmem_limit_bytes=60 * 1024 * 1024
+        ),
+    )(eri, amps, cols, occ_live, sort_in, sort_out)
+    flat = got.reshape(irreps_here, a_local * BLK, rows)
+    update = jnp.transpose(flat, (0, 2, 1))
+    energy = lax.psum_scatter(energy / (nv * BLK), "virt", scatter_dimension=1, tiled=True)
+    return (update, energy)
+
+
 def solution(mesh):
     placed = (
         P("pair", None, None, None),
@@ -77,10 +314,19 @@
         P(),
         P(),
     )
-    return jax.shard_map(
-        shards,
-        mesh=mesh,
-        in_specs=placed,
-        out_specs=(P("pair", None, "virt"), P("pair", "virt")),
-        check_vma=False,
-    )
+
+    def run(*arrays):
+        amplitudes, integrals = arrays[:2]
+        loc = integrals.shape[3] // (mesh.shape["virt"] * mesh.shape["pair"])
+        whole_slots = loc % amplitudes.shape[3] == 0
+        whole_chunks = (integrals.shape[1] // mesh.shape["virt"]) % 32 == 0
+        body = fused_shards if whole_slots and whole_chunks else shards
+        return jax.shard_map(
+            body,
+            mesh=mesh,
+            in_specs=placed,
+            out_specs=(P("pair", None, "virt"), P("pair", "virt")),
+            check_vma=False,
+        )(*arrays)
+
+    return run

time: 1330 us -> 595 us (0.45)
  waiting for transfers between devices: 574 us -> 38.8 us
  Pallas kernels: 0 us -> 477 us
  blocking collectives: 370 us -> 0 us
  local copies, waits for them, and re-layouts: 280 us -> 47.8 us
  matrix products: 59 us -> 1.22 us
  starting transfers between devices: 19.9 us -> 0.04 us
    all_to_all x3 -> x0, waiting for transfers between devices: 534 us -> none  [the longest x1 299 us: shards(): lax.all_to_all(piece, 'virt', split_axis=0, concat_axis=2, tiled=True)]
    pallas_call x0 -> x1, Pallas kernels: none -> 477 us  [fused_shards(): pl.pallas_call(functools.partial(ladder_kernel, n_virt, n_pair, irreps_he...]
    all_to_all x1 -> x0, blocking collectives: 370 us -> none  [shards(): lax.all_to_all(piece, 'virt', split_axis=0, concat_axis=2, tiled=True)]
    all_to_all x8 -> x0, local copies, waits for them, and re-layouts: 141 us -> none  [the longest x6 126 us: shards(): lax.all_to_all(piece, 'virt', split_axis=0, concat_axis=2, tiled=True)]
    dot_general x3 -> x2, matrix products: 59 us -> 1.22 us  [the longest x1 0.96 us: fused_shards(): jnp.einsum('hag,gs->hsa', b_onehot, eps_here, precision=lax.Precision.HIG...]
    transpose x2 -> x0, local copies, waits for them, and re-layouts: 28.3 us -> none  [shards(): jnp.transpose(moved, (0, 1, 3, 2, 4))]
    reshape x3 -> x4, local copies, waits for them, and re-layouts: 47.4 us -> 24.1 us  [the longest x1 21.3 us: fused_shards(): flat = got.reshape(irreps_here, a_local * BLK, rows)]
    unnamed x16 -> x3, local copies, waits for them, and re-layouts: 44.6 us -> 23.5 us
  transfers between devices with their start and end apart: 4 -> 1, of which waited for: 4 -> 1; matrix products, arithmetic and copies ran while one was open for 12% -> 4% of each run, Pallas kernels for 0% -> 0%
where the time goes in v1:
time: 595 us; the launch traced here: 593 us
  Pallas kernels  477 us (80%)
  local copies, waits for them, and re-layouts  47.8 us (8%)
  waiting for transfers between devices  38.8 us (7%)
  between operations  14.1 us (2%)
  other arithmetic  13.9 us (2%)
    pallas_call x1, Pallas kernels, fused_shards(): pl.pallas_call(functools.partial(ladder_kernel, n_virt, n_pair, irreps_he...  477 us
    unnamed x2, waiting for transfers between devices  38.8 us
    unnamed x3, local copies, waits for them, and re-layouts  23.5 us
    reshape x1, local copies, waits for them, and re-layouts, fused_shards(): flat = got.reshape(irreps_here, a_local * BLK, rows)  21.3 us
  transfers between devices with their start and end apart: 1, of which 1 were waited for; matrix products, arithmetic and copies ran while one was open for 4% of the time, Pallas kernels for 0%

profile of v1, /device:TPU:0, one launch (start us, length us, event | category | flops | bytes accessed | tf_op | source)
XLA Modules:
  0.0 593.2 jit_solution(13149286292929631215)
XLA Ops:
  7.2 0.0 reduce-scatter.4.cloned.1.call-start
  7.3 0.7 iota_compare_fusion.5
  8.0 0.9 select_reduce_fusion
  8.9 0.1 compare_convert_fusion.1
  8.9 0.1 broadcast_xor_fusion
  9.0 0.8 reshape.161
  9.8 0.1 reshape.165
  9.9 0.1 convert_element_type.32
  10.0 0.1 compare_convert_fusion
  10.0 1.7 fusion
  11.7 1.0 fusion.2
  12.7 0.3 fusion.1
  12.9 0.1 reshape.162
  13.0 0.8 fusion.4.sort_in_ref
  13.8 1.0 fusion.3.sort_out_ref
  14.8 2.0 copy.35
  16.8 21.0 %copy.32 = bf16[2,1024,2,1024]{1,3,2,0:T(8,128)(2,1)} copy(bf16[2,1024,2,1024]{3,2,1,0:T(2,128)(2,1)} %param.7) | data formatting | bytes 16777216 | tf_op args[0]
  37.8 0.6 pad_maximum_fusion.1.occ_ref
  38.4 7.4 %multiply_bitcast_fusion.amps_ref = bf16[2,2,1024,1024]{3,2,1,0:T(8,128)(2,1)} fusion(bf16[2,1024,2,1024]{1,3,2,0:T(8,128)(2,1)} %copy.32, bf16[2,1024]{1,0:T(2,128)(2,1)S(1)} %convert_element_type.32), kind=kLoop, calls=%fused_computation | loop fusion | flops 4194304 | bytes 16781312 | tf_op jit(solution)/shard_map/transpose | solution.py:240
  45.8 477.2 %shard_map.86 = (bf16[2,64,8,8,1024]{4,3,2,1,0:T(8,128)(2,1)}, bf16[8,4,2,2,64,2048]{5,4,3,2,1,0:T(8,128)(2,1)}, f32[2,1024]{1,0:T(2,128)}) custom-call(bf16[2,4096,2048]{2,1,0:T(8,128)(2,1)} %bitcast.23, bf16[2,2,1024,1024]{3,2,1,0:T(8,128)(2,1)} %multiply_bitcast_fusion.amps_ref, f32[8,512,4]{2,1,0:T(8,128)} %bitcast.26, ...), custom_call_target="tpu_custom_call" | custom-call | tf_op jit(solution)/shard_map/pallas_call | solution.py:275
  523.0 0.7 broadcast_multiply_fusion
  523.7 1.0 copy.41
  524.7 0.0 reduce-scatter.4.cloned.1.call-update
  524.8 21.3 %copy.38 = bf16[2,4096,1024]{1,2,0:T(8,128)(2,1)} copy(bf16[2,4096,1024]{2,1,0:T(8,128)(2,1)} %bitcast.24) | data formatting | bytes 33554432 | tf_op jit(solution)/shard_map/reshape | solution.py:301
  546.0 38.8 %reduce-scatter.4.cloned.1.call-done = f32[128,2]{1,0:T(8,128)} async-done(((f32[1024,2]{1,0:T(8,128)}), f32[128,2]{1,0:T(8,128)}) %reduce-scatter.4.cloned.1.call-update) | async-done | bytes 1040
  584.8 1.5 copy.42
  (8 shorter events, 0.1 us)
Async XLA Ops:
  7.2 577.7 %reduce-scatter.4.cloned.1.call-start = ((), (), s32[]{:S(2)}) async-start(), calls=%async_computation.1 | async-start | bytes 589824
Sparse Core Ops, SparseCore 0:
  524.9 59.9 reduce-scatter.3

commit v2 on v1

--- a/solution.py
+++ b/solution.py
@@ -12,6 +12,7 @@
 BLK = 64
 CS = 16
 SLABS = 2
+A_SORT = 32
 MESH = pl.DeviceIdType.MESH
 
 
@@ -84,11 +85,11 @@
 
 
 def ladder_kernel(
-    n_virt, n_pair, irreps_here, a_local, parts_sb,
+    n_virt, n_pair, irreps_here, a_chunk, cuts, depth, parts_sb, energy_scale,
     eri_ref, amps_ref, rows_ref, occ_ref, sort_in_ref, sort_out_ref,
     got_ref, recv_ref, energy_ref,
-    x_buf, stage, y_buf, out_buf,
-    x_sem, y_sem, own_sem, send_sem, recv_sem, out_sem, got_sem,
+    x_buf, stage, y_buf, out_buf, terms, parts,
+    x_sem, y_sem, own_sem, keep_sem, send_sem, recv_sem, out_sem, got_sem, term_sem, part_sem,
 ):
     me_v = lax.axis_index("virt")
     me_p = lax.axis_index("pair")
@@ -100,7 +101,9 @@
     sort_rows = sort_in_ref.shape[0]
     a_sort = sort_rows // irreps
     sb_here = n_pair * parts_sb
-    chunk_rows = a_local * irreps
+    chunk_rows = a_chunk * irreps
+    steps = n_virt * cuts
+    e_cols = nrows // n_virt
     tile_n = 512
     tile_r = 256
 
@@ -112,39 +115,53 @@
     pl.semaphore_wait(barrier, n_pair - 1 + n_virt - 1)
 
     def target(t):
-        return flip_bits(me_v, n_virt - 1 - t, n_virt)
+        return flip_bits(me_v, n_virt - 1 - t // cuts, n_virt)
 
     def pair_copy(t, d):
         peer = flip_bits(me_p, d, n_pair)
         return pltpu.make_async_remote_copy(
-            src_ref=stage.at[t % 2, peer],
+            src_ref=stage.at[t % depth, peer],
             dst_ref=recv_ref.at[t, me_p],
-            send_sem=send_sem.at[t % 2, d - 1],
+            send_sem=send_sem.at[t % depth, d - 1],
             recv_sem=recv_sem.at[t, d - 1],
             device_id=(me_v, peer),
             device_id_type=MESH,
         )
 
     def own_copy(t):
-        return pltpu.make_async_copy(stage.at[t % 2, me_p], recv_ref.at[t, me_p], own_sem.at[t % 2])
+        return pltpu.make_async_copy(stage.at[t % depth, me_p], recv_ref.at[t, me_p], own_sem.at[t % depth])
 
     def out_copy(t):
         dest = target(t)
-        if t == n_virt - 1:
-            return pltpu.make_async_copy(out_buf.at[t], got_ref.at[:, :, me_v], own_sem.at[2])
+        cut = t % cuts
+        there = got_ref.at[:, cut * a_chunk : (cut + 1) * a_chunk, me_v]
+        if t // cuts == n_virt - 1:
+            return pltpu.make_async_copy(out_buf.at[t], there, keep_sem.at[cut])
         return pltpu.make_async_remote_copy(
             src_ref=out_buf.at[t],
-            dst_ref=got_ref.at[:, :, me_v],
+            dst_ref=there,
             send_sem=out_sem.at[t],
             recv_sem=got_sem.at[t],
             device_id=(dest, me_p),
             device_id_type=MESH,
         )
 
+    def part_copy(d):
+        dest = flip_bits(me_v, d, n_virt)
+        cols = pl.ds(pl.multiple_of(dest * e_cols, e_cols), e_cols)
+        return pltpu.make_async_remote_copy(
+            src_ref=terms.at[:, cols],
+            dst_ref=parts.at[d - 1],
+            send_sem=term_sem.at[d - 1],
+            recv_sem=part_sem.at[d - 1],
+            device_id=(dest, me_p),
+            device_id_type=MESH,
+        )
+
     def prepare(t):
         dest = target(t)
         load = pltpu.make_async_copy(
-            eri_ref.at[:, pl.ds(pl.multiple_of(dest * chunk_rows, chunk_rows), chunk_rows), :], x_buf, x_sem
+            eri_ref.at[:, pl.ds(pl.multiple_of((dest * cuts + t % cuts) * chunk_rows, chunk_rows), chunk_rows), :], x_buf, x_sem
         )
         load.start()
         load.wait()
@@ -152,14 +169,14 @@
         def sort_tile(n, carry):
             cols = pl.ds(pl.multiple_of(n * tile_n, tile_n), tile_n)
             for s in range(slabs):
-                for q in range(a_local // a_sort):
+                for q in range(a_chunk // a_sort):
                     block = x_buf[s, q * sort_rows : (q + 1) * sort_rows, cols]
                     sorted_rows = jnp.dot(
                         sort_in_ref[...], block, preferred_element_type=jnp.float32
                     ).astype(jnp.bfloat16)
                     for h in range(irreps):
                         stage[
-                            t % 2, h // irreps_here, h % irreps_here, s, q * a_sort : (q + 1) * a_sort, cols
+                            t % depth, h // irreps_here, h % irreps_here, s, q * a_sort : (q + 1) * a_sort, cols
                         ] = sorted_rows[h * a_sort : (h + 1) * a_sort]
             return carry
 
@@ -189,35 +206,43 @@
                     )
                     term = jnp.dot(left, amps_ref[hh, s, :, cols], preferred_element_type=jnp.float32)
                     ladder = term if ladder is None else ladder + term
-                base = rows_ref[dest, :, hh : hh + 1]
-                live = rows_ref[dest, :, irreps_here + hh : irreps_here + hh + 1]
+                base = rows_ref[dest * cuts + t % cuts, :, hh : hh + 1]
+                live = rows_ref[dest * cuts + t % cuts, :, irreps_here + hh : irreps_here + hh + 1]
                 occ = occ_ref[hh : hh + 1, cols]
                 live_r = occ_ref[irreps_here + hh : irreps_here + hh + 1, cols]
                 denom = base - occ
                 ratio = jnp.where(live * live_r > 0.5, ladder / denom, 0.0)
-                energy_ref[hh : hh + 1, cols] += jnp.sum(ratio * ladder, axis=0, keepdims=True)
+                terms[hh : hh + 1, cols] += jnp.sum(ratio * ladder, axis=0, keepdims=True)
                 update = jnp.dot(
                     sort_out_ref[...], ratio.astype(jnp.bfloat16), preferred_element_type=jnp.float32
                 ).astype(jnp.bfloat16)
-                out_buf[t, hh, :, :, cols] = update.reshape(a_local, sb_here, tile_r)
+                out_buf[t, hh, :, :, cols] = update.reshape(a_chunk, sb_here, tile_r)
                 return carry
 
             lax.fori_loop(0, nrows // tile_r, tile, 0)
         out_copy(t).start()
 
-    energy_ref[...] = jnp.zeros_like(energy_ref)
-    prepare(0)
-    prepare(1)
-    for t in range(n_virt):
+    terms[...] = jnp.zeros_like(terms)
+    for t in range(depth):
+        prepare(t)
+    for t in range(steps):
         for d in range(1, n_pair):
             pair_copy(t, d).wait_recv()
         own_copy(t).wait()
         compute(t)
         for d in range(1, n_pair):
             pair_copy(t, d).wait_send()
-        if t + 2 < n_virt:
-            prepare(t + 2)
-    for t in range(n_virt):
+        if t + depth < steps:
+            prepare(t + depth)
+    for d in range(1, n_virt):
+        part_copy(d).start()
+    for d in range(1, n_virt):
+        part_copy(d).wait()
+    mine = terms[:, pl.ds(pl.multiple_of(me_v * e_cols, e_cols), e_cols)]
+    for d in range(1, n_virt):
+        mine = mine + parts[d - 1]
+    energy_ref[...] = mine / energy_scale
+    for t in range(steps):
         out_copy(t).wait()
 
 
@@ -228,7 +253,10 @@
     nv = integrals.shape[1]
     irreps = integrals.shape[2]
     loc = integrals.shape[3]
-    a_local = nv // n_virt
+    cuts = nv // n_virt // A_SORT
+    depth = 4
+    a_chunk = A_SORT
+    steps = n_virt * cuts
     parts_sb = loc // ks
     sb_here = n_pair * parts_sb
     me_v = lax.axis_index("virt")
@@ -251,8 +279,8 @@
     base = eps_virt[None, None, :] + eps_b
     live = live_virt.reshape(-1)[None, None, :] * live_b
     cols = jnp.concatenate([base, live], axis=0)
-    cols = cols.reshape(2 * irreps_here, sb_here, n_virt, a_local)
-    cols = jnp.transpose(cols, (2, 1, 3, 0)).reshape(n_virt, sb_here * a_local, 2 * irreps_here)
+    cols = cols.reshape(2 * irreps_here, sb_here, steps, a_chunk)
+    cols = jnp.transpose(cols, (2, 1, 3, 0)).reshape(steps, sb_here * a_chunk, 2 * irreps_here)
 
     occ_onehot = pair_list[..., None] == jnp.arange(eps_occ.shape[0], dtype=jnp.int32)
     occ_terms = jnp.sum(jnp.where(occ_onehot, eps_occ, 0.0), axis=-1)
@@ -260,47 +288,51 @@
     live_rows = jnp.arange(rows, dtype=jnp.int32)[None, :] < pick_counts(irrep_ids, pair_counts)[:, None]
     occ_live = jnp.concatenate([occ, live_rows.astype(jnp.float32)], axis=0)
 
-    a_sort = 32
+    a_sort = A_SORT
     n_in = a_sort * irreps
     i_in = jnp.arange(n_in, dtype=jnp.int32)
     from_in = (i_in % a_sort) * irreps + i_in // a_sort
     sort_in = (from_in[:, None] == i_in[None, :]).astype(jnp.bfloat16)
-    i_out = jnp.arange(a_local * sb_here, dtype=jnp.int32)
-    from_out = (i_out % sb_here) * a_local + i_out // sb_here
+    i_out = jnp.arange(a_chunk * sb_here, dtype=jnp.int32)
+    from_out = (i_out % sb_here) * a_chunk + i_out // sb_here
     sort_out = (from_out[:, None] == i_out[None, :]).astype(jnp.bfloat16)
 
     eri = integrals.reshape(slabs, nv * irreps, loc)
     vmem = pl.BlockSpec(memory_space=pltpu.VMEM)
     hbm = pl.BlockSpec(memory_space=pl.ANY)
     got, _, energy = pl.pallas_call(
-        functools.partial(ladder_kernel, n_virt, n_pair, irreps_here, a_local, parts_sb),
+        functools.partial(ladder_kernel, n_virt, n_pair, irreps_here, a_chunk, cuts, depth, parts_sb, nv * BLK),
         out_shape=(
-            jax.ShapeDtypeStruct((irreps_here, a_local, n_virt, sb_here, rows), jnp.bfloat16),
-            jax.ShapeDtypeStruct((n_virt, n_pair, irreps_here, slabs, a_local, loc), jnp.bfloat16),
-            jax.ShapeDtypeStruct((irreps_here, rows), jnp.float32),
+            jax.ShapeDtypeStruct((irreps_here, a_chunk * cuts, n_virt, sb_here, rows), jnp.bfloat16),
+            jax.ShapeDtypeStruct((steps, n_pair, irreps_here, slabs, a_chunk, loc), jnp.bfloat16),
+            jax.ShapeDtypeStruct((irreps_here, rows // n_virt), jnp.float32),
         ),
         in_specs=[hbm, vmem, vmem, vmem, vmem, vmem],
         out_specs=(hbm, hbm, vmem),
         scratch_shapes=[
-            pltpu.VMEM((slabs, a_local * irreps, loc), jnp.bfloat16),
-            pltpu.VMEM((2, n_pair, irreps_here, slabs, a_local, loc), jnp.bfloat16),
-            pltpu.VMEM((n_pair, irreps_here, slabs, a_local, loc), jnp.bfloat16),
-            pltpu.VMEM((n_virt, irreps_here, a_local, sb_here, rows), jnp.bfloat16),
+            pltpu.VMEM((slabs, a_chunk * irreps, loc), jnp.bfloat16),
+            pltpu.VMEM((depth, n_pair, irreps_here, slabs, a_chunk, loc), jnp.bfloat16),
+            pltpu.VMEM((n_pair, irreps_here, slabs, a_chunk, loc), jnp.bfloat16),
+            pltpu.VMEM((steps, irreps_here, a_chunk, sb_here, rows), jnp.bfloat16),
+            pltpu.VMEM((irreps_here, rows), jnp.float32),
+            pltpu.VMEM((n_virt - 1, irreps_here, rows // n_virt), jnp.float32),
             pltpu.SemaphoreType.DMA,
             pltpu.SemaphoreType.DMA,
-            pltpu.SemaphoreType.DMA((3,)),
-            pltpu.SemaphoreType.DMA((2, n_pair - 1)),
-            pltpu.SemaphoreType.DMA((n_virt, n_pair - 1)),
-            pltpu.SemaphoreType.DMA((n_virt,)),
-            pltpu.SemaphoreType.DMA((n_virt,)),
+            pltpu.SemaphoreType.DMA((depth,)),
+            pltpu.SemaphoreType.DMA((cuts,)),
+            pltpu.SemaphoreType.DMA((depth, n_pair - 1)),
+            pltpu.SemaphoreType.DMA((steps, n_pair - 1)),
+            pltpu.SemaphoreType.DMA((steps,)),
+            pltpu.SemaphoreType.DMA((steps,)),
+            pltpu.SemaphoreType.DMA((n_virt - 1,)),
+            pltpu.SemaphoreType.DMA((n_virt - 1,)),
         ],
         compiler_params=pltpu.CompilerParams(
             collective_id=0, has_side_effects=True, vmem_limit_bytes=60 * 1024 * 1024
         ),
     )(eri, amps, cols, occ_live, sort_in, sort_out)
-    flat = got.reshape(irreps_here, a_local * BLK, rows)
+    flat = got.reshape(irreps_here, a_chunk * cuts * BLK, rows)
     update = jnp.transpose(flat, (0, 2, 1))
-    energy = lax.psum_scatter(energy / (nv * BLK), "virt", scatter_dimension=1, tiled=True)
     return (update, energy)
 
 
@@ -319,7 +351,7 @@
         amplitudes, integrals = arrays[:2]
         loc = integrals.shape[3] // (mesh.shape["virt"] * mesh.shape["pair"])
         whole_slots = loc % amplitudes.shape[3] == 0
-        whole_chunks = (integrals.shape[1] // mesh.shape["virt"]) % 32 == 0
+        whole_chunks = (integrals.shape[1] // mesh.shape["virt"]) % A_SORT == 0
         body = fused_shards if whole_slots and whole_chunks else shards
         return jax.shard_map(
             body,

time: 595 us -> 512 us (0.86)
  waiting for transfers between devices: 38.8 us -> 0 us
  Pallas kernels: 477 us -> 450 us
  between operations: 14.1 us -> 0.72 us
    unnamed x2 -> x0, waiting for transfers between devices: 38.8 us -> none
    pallas_call x1, Pallas kernels: 477 us -> 450 us  [fused_shards(): pl.pallas_call(functools.partial(ladder_kernel, n_virt, n_pair, irreps_he...]
    unnamed x3 -> x4, local copies, waits for them, and re-layouts: 23.5 us -> 21.6 us
  transfers between devices with their start and end apart: 1 -> 0, of which waited for: 1 -> 0; matrix products, arithmetic and copies ran while one was open for 4% -> 0% of each run, Pallas kernels for 0% -> 0%
where the time goes in v2:
time: 512 us; the launch traced here: 510 us
  Pallas kernels  450 us (88%)
  local copies, waits for them, and re-layouts  46 us (9%)
  other arithmetic  12.3 us (2%)
    pallas_call x1, Pallas kernels, fused_shards(): pl.pallas_call(functools.partial(ladder_kernel, n_virt, n_pair, irreps_he...  450 us
    unnamed x4, local copies, waits for them, and re-layouts  21.6 us
    reshape x1, local copies, waits for them, and re-layouts, fused_shards(): flat = got.reshape(irreps_here, a_chunk * cuts * BLK, rows)  21.2 us

profile of v2, /device:TPU:0, one launch (start us, length us, event | category | flops | bytes accessed | tf_op | source)
XLA Modules:
  0.0 509.9 jit_solution(3584823608470588359)
XLA Ops:
  0.7 0.9 select_reduce_fusion
  1.6 0.1 compare_convert_fusion.1
  1.6 0.1 broadcast_xor_fusion
  1.7 0.8 reshape.158
  2.5 0.7 iota_compare_fusion.5
  3.2 0.1 reshape.162
  3.3 0.1 convert_element_type.32
  3.4 0.1 compare_convert_fusion
  3.4 1.7 fusion
  5.1 0.6 pad_maximum_fusion.1.occ_ref
  5.8 0.9 fusion.2
  6.7 0.3 fusion.1
  7.0 0.1 reshape.159
  7.1 0.8 fusion.3
  7.9 2.1 copy.29
  10.1 21.0 %copy.26 = bf16[2,1024,2,1024]{1,3,2,0:T(8,128)(2,1)} copy(bf16[2,1024,2,1024]{3,2,1,0:T(2,128)(2,1)} %param.7) | data formatting | bytes 16777216 | tf_op args[0]
  31.1 7.4 %multiply_bitcast_fusion.amps_ref = bf16[2,2,1024,1024]{3,2,1,0:T(8,128)(2,1)} fusion(bf16[2,1024,2,1024]{1,3,2,0:T(8,128)(2,1)} %copy.26, bf16[2,1024]{1,0:T(2,128)(2,1)S(1)} %convert_element_type.32), kind=kLoop, calls=%fused_computation | loop fusion | flops 4194304 | bytes 16781312 | tf_op jit(solution)/shard_map/transpose | solution.py:268
  38.5 449.6 %shard_map.86 = (bf16[2,64,8,8,1024]{4,3,2,1,0:T(8,128)(2,1)}, bf16[16,4,2,2,32,2048]{5,4,3,2,1,0:T(8,128)(2,1)}, f32[2,128]{1,0:T(2,128)}) custom-call(bf16[2,4096,2048]{2,1,0:T(8,128)(2,1)} %bitcast.21, bf16[2,2,1024,1024]{3,2,1,0:T(8,128)(2,1)} %multiply_bitcast_fusion.amps_ref, f32[16,256,4]{2,1,0:T(8,128)} %bitcast.24, ...), custom_call_target="tpu_custom_call" | custom-call | tf_op jit(solution)/shard_map/pallas_call | solution.py:303
  488.1 0.0 copy-start
  488.1 21.2 %copy.32 = bf16[2,4096,1024]{1,2,0:T(8,128)(2,1)} copy(bf16[2,4096,1024]{2,1,0:T(8,128)(2,1)} %bitcast.23) | data formatting | bytes 33554432 | tf_op jit(solution)/shard_map/reshape | solution.py:334
  509.3 0.0 copy-done
  509.3 0.6 copy.43
  (8 shorter events, 0.1 us)
Async XLA Ops:
  488.1 21.2 %copy-start = (f32[2,128]{1,0:T(2,128)S(1)}, f32[2,128]{1,0:T(2,128)}, u32[]{:S(2)}) copy-start(f32[2,128]{1,0:T(2,128)} %get-tuple-element.17) | copy-start | bytes 3076

commit v3 on v2

--- a/solution.py
+++ b/solution.py
@@ -84,9 +84,17 @@
     return flipped
 
 
+def send_order(count):
+    half, quarter = count // 2, count // 4
+    far = list(range(count - 1, half - 1, -1))
+    near = list(range(half - 1, -1, -1))
+    mixed = [d for both in zip(far[:quarter], near[:quarter]) for d in both]
+    return mixed + far[quarter:] + near[quarter:]
+
+
 def ladder_kernel(
     n_virt, n_pair, irreps_here, a_chunk, cuts, depth, parts_sb, energy_scale,
-    eri_ref, amps_ref, rows_ref, occ_ref, sort_in_ref, sort_out_ref,
+    eri_ref, amps_ref, dmask_ref, rows_ref, occ_ref, sort_in_ref, sort_out_ref,
     got_ref, recv_ref, energy_ref,
     x_buf, stage, y_buf, out_buf, terms, parts,
     x_sem, y_sem, own_sem, keep_sem, send_sem, recv_sem, out_sem, got_sem, term_sem, part_sem,
@@ -103,6 +111,7 @@
     sb_here = n_pair * parts_sb
     chunk_rows = a_chunk * irreps
     steps = n_virt * cuts
+    order = send_order(n_virt)
     e_cols = nrows // n_virt
     tile_n = 512
     tile_r = 256
@@ -115,7 +124,7 @@
     pl.semaphore_wait(barrier, n_pair - 1 + n_virt - 1)
 
     def target(t):
-        return flip_bits(me_v, n_virt - 1 - t // cuts, n_virt)
+        return flip_bits(me_v, order[t // cuts], n_virt)
 
     def pair_copy(t, d):
         peer = flip_bits(me_p, d, n_pair)
@@ -135,7 +144,7 @@
         dest = target(t)
         cut = t % cuts
         there = got_ref.at[:, cut * a_chunk : (cut + 1) * a_chunk, me_v]
-        if t // cuts == n_virt - 1:
+        if order[t // cuts] == 0:
             return pltpu.make_async_copy(out_buf.at[t], there, keep_sem.at[cut])
         return pltpu.make_async_remote_copy(
             src_ref=out_buf.at[t],
@@ -204,6 +213,7 @@
                         ],
                         axis=0,
                     )
+                    left = left * dmask_ref[hh : hh + 1, :]
                     term = jnp.dot(left, amps_ref[hh, s, :, cols], preferred_element_type=jnp.float32)
                     ladder = term if ladder is None else ladder + term
                 base = rows_ref[dest * cuts + t % cuts, :, hh : hh + 1]
@@ -264,8 +274,7 @@
     slots = jnp.arange(BLK, dtype=jnp.int32)
     live_d = slots[None, :] < pick_counts(irrep_ids, virt_counts)[:, None]
     dmask = jnp.tile(live_d, (1, ks // BLK)).astype(jnp.bfloat16)
-    masked = amplitudes * dmask[:, None, None, :]
-    amps = jnp.transpose(masked, (0, 2, 3, 1))
+    amps = jnp.transpose(amplitudes, (0, 2, 3, 1))
 
     a_index = jnp.arange(nv, dtype=jnp.int32)
     a_irrep = a_index // BLK
@@ -307,7 +316,7 @@
             jax.ShapeDtypeStruct((steps, n_pair, irreps_here, slabs, a_chunk, loc), jnp.bfloat16),
             jax.ShapeDtypeStruct((irreps_here, rows // n_virt), jnp.float32),
         ),
-        in_specs=[hbm, vmem, vmem, vmem, vmem, vmem],
+        in_specs=[hbm, vmem, vmem, vmem, vmem, vmem, vmem],
         out_specs=(hbm, hbm, vmem),
         scratch_shapes=[
             pltpu.VMEM((slabs, a_chunk * irreps, loc), jnp.bfloat16),
@@ -330,7 +339,7 @@
         compiler_params=pltpu.CompilerParams(
             collective_id=0, has_side_effects=True, vmem_limit_bytes=60 * 1024 * 1024
         ),
-    )(eri, amps, cols, occ_live, sort_in, sort_out)
+    )(eri, amps, dmask, cols, occ_live, sort_in, sort_out)
     flat = got.reshape(irreps_here, a_chunk * cuts * BLK, rows)
     update = jnp.transpose(flat, (0, 2, 1))
     return (update, energy)

time: 512 us -> 504 us (0.984)
  other arithmetic: 12.3 us -> 4.96 us
    transpose x1 -> x0, other arithmetic: 7.39 us -> none  [fused_shards(): amps = jnp.transpose(masked, (0, 2, 3, 1))]
where the time goes in v3:
time: 504 us; the launch traced here: 501 us
  Pallas kernels  448 us (89%)
  local copies, waits for them, and re-layouts  46.6 us (9%)
    pallas_call x1, Pallas kernels, fused_shards(): pl.pallas_call(functools.partial(ladder_kernel, n_virt, n_pair, irreps_he...  448 us
    unnamed x4, local copies, waits for them, and re-layouts  21.6 us
    reshape x1, local copies, waits for them, and re-layouts, fused_shards(): flat = got.reshape(irreps_here, a_chunk * cuts * BLK, rows)  21.2 us

profile of v3, /device:TPU:0, one launch (start us, length us, event | category | flops | bytes accessed | tf_op | source)
XLA Modules:
  0.0 501.1 jit_solution(16734575661655518635)
XLA Ops:
  0.7 0.9 select_reduce_fusion
  1.6 0.1 compare_convert_fusion.1
  1.6 0.1 broadcast_xor_fusion
  1.7 0.8 reshape.151
  2.5 0.7 iota_compare_fusion.5
  3.2 0.1 reshape.155
  3.3 0.7 convert_element_type.26.dmask_ref
  4.0 0.1 compare_convert_fusion
  4.0 1.7 fusion
  5.7 0.6 pad_maximum_fusion.1.occ_ref
  6.3 0.9 fusion.2
  7.3 0.3 fusion.1
  7.6 0.1 reshape.152
  7.7 0.8 fusion.3
  8.5 2.1 copy.29
  10.7 21.0 %copy.26 = bf16[2,1024,2,1024]{1,3,2,0:T(8,128)(2,1)} copy(bf16[2,1024,2,1024]{3,2,1,0:T(2,128)(2,1)} %param.7) | data formatting | bytes 16777216 | tf_op args[0]
  31.7 447.6 %shard_map.86 = (bf16[2,64,8,8,1024]{4,3,2,1,0:T(8,128)(2,1)}, bf16[16,4,2,2,32,2048]{5,4,3,2,1,0:T(8,128)(2,1)}, f32[2,128]{1,0:T(2,128)}) custom-call(bf16[2,4096,2048]{2,1,0:T(8,128)(2,1)} %bitcast.20, bf16[2,2,1024,1024]{3,2,1,0:T(8,128)(2,1)} %bitcast.21, bf16[2,1024]{1,0:T(2,128)(2,1)} %convert_element_type.26.dmask_ref, f32[16,256,4]{2,1,0:T(8,128)} %bitcast.24, ...), custom_call_target="tpu_custom_call" | custom-call | tf_op jit(solution)/shard_map/pallas_call | solution.py:312
  479.3 0.0 copy-start
  479.3 21.2 %copy.32 = bf16[2,4096,1024]{1,2,0:T(8,128)(2,1)} copy(bf16[2,4096,1024]{2,1,0:T(8,128)(2,1)} %bitcast.23) | data formatting | bytes 33554432 | tf_op jit(solution)/shard_map/reshape | solution.py:343
  500.5 0.0 copy-done
  500.5 0.6 copy.43
  (8 shorter events, 0.1 us)
Async XLA Ops:
  479.3 21.2 %copy-start = (f32[2,128]{1,0:T(2,128)S(1)}, f32[2,128]{1,0:T(2,128)}, u32[]{:S(2)}) copy-start(f32[2,128]{1,0:T(2,128)} %get-tuple-element.17) | copy-start | bytes 3076
